TPU v7x, 32 devices: a whole 2x2x4 slice. The times are simulated.
32 devices in a mesh: seq: 8 (over z, y), dp: 4 (over x, core).
Axes of the slice: x: 2, y: 2, z: 4, core: 2. Of those that a mesh axis runs over, the one named last changes fastest.
Arguments:
- block_input: bfloat16 [4, 1024, 1536], P('dp', 'seq'), may hold values from -6 to 6
- query_proj: bfloat16 [4, 1024, 768], P('dp', 'seq'), may hold values from -8 to 8
- key_proj: bfloat16 [4, 1024, 768], P('dp', 'seq'), may hold values from -8 to 8
- value_proj: bfloat16 [4, 1024, 768], P('dp', 'seq'), may hold values from -6 to 6
- lengths: int32 [4], P('dp'), may hold values from 256 to 1024, as said below
- out_proj: bfloat16 [1536, 768], replicated, may hold values from -0.21875 to 0.21875
- kernel: float32 [31, 1536], replicated, may hold values from -1 to 1
- conv_bias: float32 [1536], replicated, may hold values from -3 to 3
- grad_output: bfloat16 [4, 1024, 1536], P('dp', 'seq'), may hold values from -6 to 6
Outputs:
- block_output: bfloat16 [4, 1024, 1536], P('dp', 'seq')
- grad_input: bfloat16 [4, 1024, 1536], P('dp', 'seq')
- grad_query: bfloat16 [4, 1024, 768], P('dp', 'seq')
- grad_out_proj: float32 [1536, 768], P('seq')
- grad_kernel: float32 [31, 1536], P(None, 'seq')
- grad_bias: float32 [1536], P('seq')
Inputs may be any that keep to these rules, and one draw needn't show every extreme that they name: `lengths`: frames at or after an utterance's length are padding; in every draw at least one utterance has all 1024 frames valid.
All inputs are finite; a program needn't handle non-finite values.
Results may differ from a plain program's by a relative error of at most 0.012.
The roundings to bfloat16 on the way count: a program that leaves them out, or rounds other values in their place, can miss the bound.
Values may be sent and summed in bfloat16 or wider, within the bound.
No kernel may reach another device: no remote copies, remote signals or barrier semaphores. Data moves between devices by JAX's collectives and lax.ppermute only.
A program may use at most 128 MiB of HBM per device.

v0:
```python
import math
import jax
import jax.numpy as jnp
from jax import lax
from jax.sharding import PartitionSpec as P

D = 1536
H = 8
HS = 96
KW = 31
HD = 768


def with_halo(x, sides, width):
    for axis, dim in sides:
        size, length = (lax.axis_size(axis), x.shape[dim])
        up = [(i, (i + 1) % size) for i in range(size - 1)]
        down = [(j, i) for i, j in up]
        last = lax.slice_in_dim(x, length - width, length, axis=dim)
        leading = lax.slice_in_dim(x, 0, width, axis=dim)
        before = lax.ppermute(last, axis, up)
        after = lax.ppermute(leading, axis, down)
        x = jnp.concatenate([before, x, after], axis=dim)
    return x


def forward_rows(query_one, key_one, value_one, key_valid, score_scale):
    row_total = query_one.shape[0]
    block_rows = math.gcd(row_total, 512)
    query_blocks = query_one.reshape(row_total // block_rows, block_rows, query_one.shape[1])

    def forward_one_block(query_block):
        scores = (
            lax.dot_general(
                query_block, key_one, (((1,), (1,)), ((), ())), preferred_element_type=jnp.float32
            )
            * score_scale
        )
        scores = jnp.where(key_valid[None, :], scores, -jnp.inf)
        row_top = jnp.max(scores, axis=-1, keepdims=True)
        log_total = row_top + jnp.log(jnp.sum(jnp.exp(scores - row_top), axis=-1, keepdims=True))
        weights = jnp.exp(scores - log_total).astype(jnp.bfloat16)
        return (jnp.dot(weights, value_one, preferred_element_type=jnp.float32), log_total[:, 0])

    outputs, log_totals = lax.map(forward_one_block, query_blocks)
    return (outputs.reshape(row_total, query_one.shape[1]), log_totals.reshape(row_total))


def backward_rows(
    query_one, key_one, value_one, grad_one, lse_one, delta_one, key_valid, score_scale
):
    row_total = query_one.shape[0]
    block_rows = math.gcd(row_total, 512)
    block_count = row_total // block_rows
    width = query_one.shape[1]

    def backward_one_block(items):
        query_block, grad_block, lse_block, delta_block = items
        scores = (
            lax.dot_general(
                query_block, key_one, (((1,), (1,)), ((), ())), preferred_element_type=jnp.float32
            )
            * score_scale
        )
        scores = jnp.where(key_valid[None, :], scores, -jnp.inf)
        probs = jnp.exp(scores - lse_block[:, None])
        grad_prob = lax.dot_general(
            grad_block, value_one, (((1,), (1,)), ((), ())), preferred_element_type=jnp.float32
        )
        grad_score = (probs * (grad_prob - delta_block[:, None])).astype(jnp.bfloat16)
        return jnp.dot(grad_score, key_one, preferred_element_type=jnp.float32) * score_scale

    results = lax.map(
        backward_one_block,
        (
            query_one.reshape(block_count, block_rows, width),
            grad_one.reshape(block_count, block_rows, width),
            lse_one.reshape(block_count, block_rows),
            delta_one.reshape(block_count, block_rows),
        ),
    )
    return results.reshape(row_total, width)


def on_device(
    block_input, query_proj, key_proj, value_proj, lengths, out_proj, kernel, conv_bias, grad_output
):
    frames_dev = block_input.shape[1]
    seq_count = lax.axis_size("seq")
    total_frames = frames_dev * seq_count
    first_frame = lax.axis_index("seq") * frames_dev
    utt_length = lengths[0]
    local_valid = first_frame + jnp.arange(frames_dev) < utt_length
    all_valid = jnp.arange(total_frames) < utt_length
    score_scale = 1.0 / math.sqrt(HS)
    halo_width = KW // 2
    group_size = seq_count // H
    sub_rows = frames_dev // group_size
    query_local = query_proj[0]

    def to_serving(matrix):
        return matrix.reshape(frames_dev, H, HS).transpose(1, 0, 2).reshape(seq_count, sub_rows, HS)

    def from_serving(returned):
        return returned.reshape(H, frames_dev, HS).transpose(1, 0, 2).reshape(frames_dev, HD)

    query_mine = lax.all_to_all(
        to_serving(query_local), "seq", split_axis=0, concat_axis=1, tiled=True
    )[0]
    key_send = jnp.repeat(
        key_proj[0].reshape(frames_dev, H, HS).transpose(1, 0, 2), group_size, axis=0
    )
    value_send = jnp.repeat(
        value_proj[0].reshape(frames_dev, H, HS).transpose(1, 0, 2), group_size, axis=0
    )
    key_mine, value_mine = (
        lax.all_to_all(key_send, "seq", split_axis=0, concat_axis=1, tiled=True),
        lax.all_to_all(value_send, "seq", split_axis=0, concat_axis=1, tiled=True),
    )
    key_mine = key_mine[0]
    value_mine = value_mine[0]
    head_out, head_lse = forward_rows(query_mine, key_mine, value_mine, all_valid, score_scale)
    head_attended = head_out.astype(jnp.bfloat16)
    attended = from_serving(
        lax.all_to_all(head_attended[None], "seq", split_axis=1, concat_axis=0, tiled=True)
    )
    projected = lax.dot_general(
        attended, out_proj, (((1,), (1,)), ((), ())), preferred_element_type=jnp.float32
    )
    mixed_rows = (block_input[0].astype(jnp.float32) + projected).astype(jnp.bfloat16)
    masked = jnp.where(local_valid[:, None], mixed_rows, jnp.zeros_like(mixed_rows))
    padded = with_halo(masked, (("seq", 0),), halo_width).astype(jnp.float32)
    conv_rows = jnp.broadcast_to(conv_bias, (frames_dev, D))
    for tap in range(KW):
        conv_rows = conv_rows + kernel[tap] * padded[tap : tap + frames_dev]
    gate_rows = jax.nn.sigmoid(conv_rows)
    block_output = jnp.where(
        local_valid[:, None], mixed_rows.astype(jnp.float32) + conv_rows * gate_rows, 0.0
    ).astype(jnp.bfloat16)
    grad_rows = jnp.where(local_valid[:, None], grad_output[0].astype(jnp.float32), 0.0)
    grad_conv = grad_rows * gate_rows * (1.0 + conv_rows * (1.0 - gate_rows))
    kernel_local = jnp.stack(
        [jnp.sum(grad_conv * padded[tap : tap + frames_dev], axis=0) for tap in range(KW)]
    )
    bias_local = jnp.sum(grad_conv, axis=0)
    grad_padded = with_halo(grad_conv, (("seq", 0),), halo_width)
    grad_masked = jnp.zeros((frames_dev, D), jnp.float32)
    for tap in range(KW):
        begin = 2 * halo_width - tap
        grad_masked = grad_masked + kernel[tap] * grad_padded[begin : begin + frames_dev]
    grad_input = (grad_rows + jnp.where(local_valid[:, None], grad_masked, 0.0)).astype(
        jnp.bfloat16
    )
    grad_attn = jnp.dot(grad_input, out_proj, preferred_element_type=jnp.float32).astype(
        jnp.bfloat16
    )
    grad_mine = lax.all_to_all(
        to_serving(grad_attn), "seq", split_axis=0, concat_axis=1, tiled=True
    )[0]
    delta_mine = jnp.sum(grad_mine.astype(jnp.float32) * head_attended.astype(jnp.float32), axis=-1)
    grad_q_mine = backward_rows(
        query_mine, key_mine, value_mine, grad_mine, head_lse, delta_mine, all_valid, score_scale
    ).astype(jnp.bfloat16)
    grad_query = from_serving(
        lax.all_to_all(grad_q_mine[None], "seq", split_axis=1, concat_axis=0, tiled=True)
    )
    term_block = lax.dot_general(
        grad_input, attended, (((0,), (0,)), ((), ())), preferred_element_type=jnp.float32
    )
    partial_rows = lax.psum_scatter(term_block, "seq", scatter_dimension=0, tiled=True)
    summed = lax.psum(partial_rows.astype(jnp.bfloat16), "dp").astype(jnp.float32)
    kernel_total, bias_total = lax.psum((kernel_local, bias_local), ("seq", "dp"))
    shard_width = D // seq_count
    offset = lax.axis_index("seq") * shard_width
    grad_kernel = lax.dynamic_slice_in_dim(kernel_total, offset, shard_width, 1)
    grad_bias = lax.dynamic_slice_in_dim(bias_total, offset, shard_width, 0)
    return (block_output[None], grad_input[None], grad_query[None], summed, grad_kernel, grad_bias)


def solution(mesh):
    placed = (
        P("dp", "seq", None),
        P("dp", "seq", None),
        P("dp", "seq", None),
        P("dp", "seq", None),
        P("dp"),
        P(),
        P(),
        P(),
        P("dp", "seq", None),
    )
    return jax.shard_map(
        on_device,
        mesh=mesh,
        in_specs=placed,
        out_specs=(
            P("dp", "seq", None),
            P("dp", "seq", None),
            P("dp", "seq", None),
            P("seq", None),
            P(None, "seq"),
            P("seq"),
        ),
        check_vma=False,
    )
```

profile of v0, /device:TPU:0, one launch (start us, length us, event | category | flops | bytes accessed | tf_op | source)
XLA Modules:
  0.0 321.5 jit_solution(12944451114000263372)
XLA Ops:
  9.9 7.3 %all-to-all-start = ((bf16[8,128,96]{1,2,0:T(8,128)(2,1)}), bf16[8,128,96]{1,2,0:T(8,128)(2,1)S(1)}, u32[]{:S(2)}, u32[]{:S(2)}) async-start(bf16[8,128,96]{1,2,0:T(8,128)(2,1)} %bitcast.3), calls=%async_computation | async-start | bytes 393216 | tf_op jit(solution)/shard_map/all_to_all | solution.py:107
  18.9 6.2 %all-to-all-done = bf16[8,128,96]{1,2,0:T(8,128)(2,1)S(1)} async-done(((bf16[8,128,96]{1,2,0:T(8,128)(2,1)}), bf16[8,128,96]{1,2,0:T(8,128)(2,1)S(1)}, u32[]{:S(2)}, u32[]{:S(2)}) %all-to-all-start) | async-done | bytes 196640 | tf_op jit(solution)/shard_map/all_to_all | solution.py:107
  25.1 3.4 %all-to-all-start.1 = ((bf16[8,128,96]{1,2,0:T(8,128)(2,1)}), bf16[8,128,96]{1,2,0:T(8,128)(2,1)S(1)}, u32[]{:S(2)}, u32[]{:S(2)}) async-start(bf16[8,128,96]{1,2,0:T(8,128)(2,1)} %bitcast.5), calls=%async_computation.1 | async-start | bytes 393216 | tf_op jit(solution)/shard_map/all_to_all | solution.py:117
  30.3 6.0 %all-to-all-done.1 = bf16[8,128,96]{1,2,0:T(8,128)(2,1)S(1)} async-done(((bf16[8,128,96]{1,2,0:T(8,128)(2,1)}), bf16[8,128,96]{1,2,0:T(8,128)(2,1)S(1)}, u32[]{:S(2)}, u32[]{:S(2)}) %all-to-all-start.1) | async-done | bytes 196640 | tf_op jit(solution)/shard_map/all_to_all | solution.py:117
  36.3 3.4 %all-to-all-start.2 = ((bf16[8,128,96]{1,2,0:T(8,128)(2,1)}), bf16[8,128,96]{1,2,0:T(8,128)(2,1)S(1)}, u32[]{:S(2)}, u32[]{:S(2)}) async-start(bf16[8,128,96]{1,2,0:T(8,128)(2,1)} %bitcast.7), calls=%async_computation.2 | async-start | bytes 393216 | tf_op jit(solution)/shard_map/all_to_all | solution.py:118
  40.0 7.3 %all-to-all-done.2 = bf16[8,128,96]{1,2,0:T(8,128)(2,1)S(1)} async-done(((bf16[8,128,96]{1,2,0:T(8,128)(2,1)}), bf16[8,128,96]{1,2,0:T(8,128)(2,1)S(1)}, u32[]{:S(2)}, u32[]{:S(2)}) %all-to-all-start.2) | async-done | bytes 196640 | tf_op jit(solution)/shard_map/all_to_all | solution.py:118
  47.6 4.6 %while.24 = (s32[]{:T(128)}, bf16[2,512,96]{1,2,0:T(8,128)(2,1)S(1)}, f32[2,512]{1,0:T(2,128)S(1)}, bf16[2,512,96]{2,1,0:T(8,128)(2,1)S(1)}, bf16[1024,96]{1,0:T...) while((s32[]{:T(128)}, ...), condition=%wide.region_3.4_spmd.clone, body=%wide.region_0.3_spmd.clone.sunk | while | flops 204997120 | bytes 7164021 | solution.py:45
  53.2 2.6 reshape.122
  56.3 3.7 %reduce.63 = bf16[1024,96]{1,0:T(8,128)(2,1)} reduce(bf16[1024,1,96]{2,1,0:T(2,128)(2,1)} %bitcast.115, bf16[]{:T(256)} %broadcast.73), dimensions={1}, to_apply=%bitcast.66.reduce_sub_computation | reduce | bytes 393218
  62.1 3.4 %all-to-all-start.3 = ((bf16[8,2,6144]{2,1,0:T(2,128)(2,1)}), bf16[8,2,6144]{2,1,0:T(2,128)(2,1)S(1)}, u32[]{:S(2)}, u32[]{:S(2)}) async-start(bf16[8,2,6144]{2,1,0:T(2,128)(2,1)} %reshape.155), calls=%async_computation.3 | async-start | bytes 393216 | tf_op jit(solution)/shard_map/all_to_all | solution.py:125
  66.8 2.5 slice_reduce_fusion.30
  69.3 3.9 %all-to-all-done.3 = bf16[8,2,6144]{2,1,0:T(2,128)(2,1)S(1)} async-done(((bf16[8,2,6144]{2,1,0:T(2,128)(2,1)}), bf16[8,2,6144]{2,1,0:T(2,128)(2,1)S(1)}, u32[]{:S(2)}, u32[]{:S(2)}) %all-to-all-start.3) | async-done | bytes 196640 | tf_op jit(solution)/shard_map/all_to_all | solution.py:125
  75.9 2.7 broadcast_select_fusion
  83.5 3.0 collective-permute-done.1
  86.9 7.5 %multiply_reduce_fusion = (f32[1536]{0:T(1024)}, f32[1536]{0:T(1024)}, f32[1536]{0:T(1024)}, f32[1536]{0:T(1024)}, f32[1536]{0:T(1024)}, /*index=5*/f32[1536]{0:...) fusion(f32[158,1536]{1,0:T(8,128)S(1)} %maximum_convert_fusion,, ...), kind=kLoop, calls=%fused_computation.190 | loop fusion | flops 21206016 | bytes 26652800 | tf_op jit(solution)/shard_map/reduce_sum | solution.py:143
  95.7 5.0 %collective-permute-start.3 = (f32[15,1536]{1,0:T(8,128)S(1)}, f32[15,1536]{1,0:T(8,128)S(1)}, u32[]{:S(2)}, u32[]{:S(2)}) collective-permute-start(f32[15,1536]{1,0:T(8,128)S(1)} %get-tuple-element.306), channel_id=1, source_target_pairs={{0,4},{4,8},{8,12},{12,16},{16,20},{20,24},{24,28},{1,5},{5,9},{9,... | collective-permute-start | bytes 276488 | tf_op jit(solution)/shard_map/ppermute | solution.py:21
  102.7 3.7 %fusion.37 = bf16[128,1536]{1,0:T(8,128)(2,1)S(1)} fusion(f32[128,1536]{1,0:T(8,128)S(1)} %get-tuple-element.299, f32[15,1536]{1,0:T(8,128)S(1)} %collective-permute-done.3, f32[15,1536]{1,0:T(8,128)S(1)} %collective-permute-done.2, bf16[1,128,1536]{2,1,0:T(8,128)(2,1)S(1)} %copy-done.11, f32[1536]{0:T(1024)S(1)} %get-tuple-element.265, ...), kind=kLoop, calls=%fused_computation.100 | loop fusion | flops 18874368 | bytes 1947776 | tf_op jit(solution)/shard_map/convert_element_type | solution.py:151
  107.2 2.9 fusion.130
  111.1 2.1 reshape.121
  115.5 6.7 %all-to-all-start.4 = ((bf16[8,128,96]{1,2,0:T(8,128)(2,1)}), bf16[8,128,96]{1,2,0:T(8,128)(2,1)S(1)}, u32[]{:S(2)}, u32[]{:S(2)}) async-start(bf16[8,128,96]{1,2,0:T(8,128)(2,1)} %bitcast.121), calls=%async_computation.4 | async-start | bytes 393216 | tf_op jit(solution)/shard_map/all_to_all | solution.py:157
  122.4 3.0 multiply_reduce_fusion.18
  128.9 3.5 %stack.127 = f32[31,1536]{1,0:T(8,128)} concatenate(f32[1,1536]{1,0:T(1,128)} %stack.96, f32[1,1536]{1,0:T(1,128)} %stack.97, f32[1,1536]{1,0:T(1,128)} %stack.98, f32[1,1536]{1,0:T(1,128)} %stack.99, f32[1,1536]{1,0:T(1,128)} %stack.100, f32[1,1536]{1,0:T(1,128)S(1)} %stack.101, f32[1,1536]{1,0:T(1,128)S(1)} %stack.102, f32[1,1536]{1,0:T(1,128)S(1)} %stack.103, ...), dimensions={0} | concatenate | bytes 380928 | tf_op jit(solution)/shard_map/stack | solution.py:142
  136.5 12.9 %while.25 = (s32[]{:T(128)}, bf16[2,512,96]{1,2,0:T(8,128)(2,1)}, bf16[2,512,96]{2,1,0:T(8,128)(2,1)S(1)}, bf16[1024,96]{1,0:T(8,128)(2,1)S(1)}, f32[2,512]{1,0:...) while((s32[]{:T(128)}, bf16[2,512,96]{1,2,0:T(8,128)(2,1)}, ...), condition=%wide.region_6.7_spmd.clone, body=%wide.region_5.6_spmd.clone.sunk | while | flops 305185792 | bytes 6241429 | solution.py:73
  139.8 3.3 %fusion.163 = bf16[2,512,96]{1,2,0:T(8,128)(2,1)} fusion(bf16[2,512,96]{1,2,0:T(8,128)(2,1)} %get-tuple-element.455, s32[]{:T(128)S(6)} %copy.133, bf16[1024,96]{1,0:T(8,128)(2,1)S(1)} %get-tuple-element.467, f32[512,1024]{1,0:T(8,128)} %fusion.162, bf16[1024,96]{1,0:T(8,128)(2,1)S(1)} %get-tuple-element.470, f32[512]{0:T(512)S(1)} %bitcast.129, ...), kind=kOutput, calls=%fused_computation.17.clone.1 | convolution fusion | flops 204521472 | bytes 2955264 | tf_op jit(solution)/shard_map/while/body/eval_jaxpr/dot_general | solution.py:71
  146.2 3.2 fusion.163
  151.3 2.7 reshape.123
  154.0 3.7 %reduce.64 = bf16[1024,96]{1,0:T(8,128)(2,1)} reduce(bf16[1024,1,96]{2,1,0:T(2,128)(2,1)} %bitcast.116, bf16[]{:T(256)} %broadcast.73), dimensions={1}, to_apply=%bitcast.68.reduce_sub_computation | reduce | bytes 393218
  159.8 4.5 %all-to-all-start.5 = ((bf16[8,2,6144]{2,1,0:T(2,128)(2,1)}), bf16[8,2,6144]{2,1,0:T(2,128)(2,1)}, u32[]{:S(2)}, u32[]{:S(2)}) async-start(bf16[8,2,6144]{2,1,0:T(2,128)(2,1)} %reshape.157), calls=%async_computation.5 | async-start | bytes 393216 | tf_op jit(solution)/shard_map/all_to_all | solution.py:165
  164.3 48.2 %reduce-scatter.2.cloned.1.call-done = f32[192,768]{1,0:T(8,128)} async-done(((f32[1536,768]{1,0:T(8,128)}), f32[192,768]{1,0:T(8,128)}) %reduce-scatter.2.cloned.1.call-update) | async-done | bytes 589840 | tf_op jit(solution)/shard_map/reduce_scatter | solution.py:170
  215.4 40.3 %psum.23 = f32[1536]{0:T(1024)S(1)} all-reduce(f32[1536]{0:T(1024)S(1)} %copy-done.48), channel_id=1, replica_groups=mesh['seq'=8,'dp'=4] {'seq','dp'}, use_global_device_ids=true, to_apply=%region_42.43 | all-reduce | flops 1536 | bytes 12288 | tf_op jit(solution)/shard_map/psum | solution.py:172
  256.4 20.2 %all-reduce.5.cloned.1.call-done = f32[31,1536]{1,0:T(8,128)} async-done(((f32[31,1536]{1,0:T(8,128)}), f32[31,1536]{1,0:T(8,128)}) %all-reduce.5.cloned.1.call-update) | async-done | bytes 190480 | tf_op jit(solution)/shard_map/psum | solution.py:172
  280.6 31.7 %all-reduce.3.cloned.1.call-done = bf16[192,768]{1,0:T(8,128)(2,1)} async-done(((bf16[192,768]{1,0:T(8,128)(2,1)}), bf16[192,768]{1,0:T(8,128)(2,1)}) %all-reduce.3.cloned.1.call-update) | async-done | bytes 294928 | tf_op jit(solution)/shard_map/psum | solution.py:171
  (210 shorter events, 56.5 us)
Async XLA Ops:
  8.0 67.7 %copy-start = (bf16[1536,768]{1,0:T(8,128)(2,1)S(1)}, bf16[1536,768]{1,0:T(8,128)(2,1)}, u32[]{:S(2)}) copy-start(bf16[1536,768]{1,0:T(8,128)(2,1)} %param.18) | copy-start | bytes 7077892
  9.9 15.2 %all-to-all-start = ((bf16[8,128,96]{1,2,0:T(8,128)(2,1)}), bf16[8,128,96]{1,2,0:T(8,128)(2,1)S(1)}, u32[]{:S(2)}, u32[]{:S(2)}) async-start(bf16[8,128,96]{1,2,0:T(8,128)(2,1)} %bitcast.3), calls=%async_computation | async-start | bytes 393216 | tf_op jit(solution)/shard_map/all_to_all | solution.py:107
  25.1 11.1 %all-to-all-start.1 = ((bf16[8,128,96]{1,2,0:T(8,128)(2,1)}), bf16[8,128,96]{1,2,0:T(8,128)(2,1)S(1)}, u32[]{:S(2)}, u32[]{:S(2)}) async-start(bf16[8,128,96]{1,2,0:T(8,128)(2,1)} %bitcast.5), calls=%async_computation.1 | async-start | bytes 393216 | tf_op jit(solution)/shard_map/all_to_all | solution.py:117
  36.3 11.1 %all-to-all-start.2 = ((bf16[8,128,96]{1,2,0:T(8,128)(2,1)}), bf16[8,128,96]{1,2,0:T(8,128)(2,1)S(1)}, u32[]{:S(2)}, u32[]{:S(2)}) async-start(bf16[8,128,96]{1,2,0:T(8,128)(2,1)} %bitcast.7), calls=%async_computation.2 | async-start | bytes 393216 | tf_op jit(solution)/shard_map/all_to_all | solution.py:118
  52.2 14.0 %copy-start.49 = (f32[2,512]{1,0:T(2,128)}, f32[2,512]{1,0:T(2,128)S(1)}, u32[]{:S(2)}) copy-start(f32[2,512]{1,0:T(2,128)S(1)} %get-tuple-element.448) | copy-start | bytes 12292
  52.3 23.3 %copy-start.1 = (bf16[1024,96]{1,0:T(8,128)(2,1)}, bf16[1024,96]{1,0:T(8,128)(2,1)S(1)}, u32[]{:S(2)}) copy-start(bf16[1024,96]{1,0:T(8,128)(2,1)S(1)} %get-tuple-element.477) | copy-start | bytes 589828
  52.3 23.3 %copy-start.3 = (bf16[1024,96]{1,0:T(8,128)(2,1)}, bf16[1024,96]{1,0:T(8,128)(2,1)S(1)}, u32[]{:S(2)}) copy-start(bf16[1024,96]{1,0:T(8,128)(2,1)S(1)} %get-tuple-element.480) | copy-start | bytes 589828
  52.3 23.3 %copy-start.5 = (bf16[2,512,96]{2,1,0:T(8,128)(2,1)}, bf16[2,512,96]{2,1,0:T(8,128)(2,1)S(1)}, u32[]{:S(2)}) copy-start(bf16[2,512,96]{2,1,0:T(8,128)(2,1)S(1)} %get-tuple-element.481) | copy-start | bytes 589828
  62.1 11.1 %all-to-all-start.3 = ((bf16[8,2,6144]{2,1,0:T(2,128)(2,1)}), bf16[8,2,6144]{2,1,0:T(2,128)(2,1)S(1)}, u32[]{:S(2)}, u32[]{:S(2)}) async-start(bf16[8,2,6144]{2,1,0:T(2,128)(2,1)} %reshape.155), calls=%async_computation.3 | async-start | bytes 393216 | tf_op jit(solution)/shard_map/all_to_all | solution.py:125
  65.5 147.0 %reduce-scatter.2.cloned.1.call-start = ((), (), s32[]{:S(2)}) async-start(), calls=%async_computation.7 | async-start | bytes 5308416 | tf_op jit(solution)/shard_map/reduce_scatter | solution.py:170
  75.7 11.0 %copy-start.11 = (bf16[1,128,1536]{2,1,0:T(8,128)(2,1)S(1)}, bf16[1,128,1536]{2,1,0:T(8,128)(2,1)}, u32[]{:S(2)}) copy-start(bf16[1,128,1536]{2,1,0:T(8,128)(2,1)} %param.21) | copy-start | bytes 1179652
  75.7 11.0 %copy-start.13 = (f32[1536]{0:T(1024)S(1)}, f32[1536]{0:T(1024)}, u32[]{:S(2)}) copy-start(f32[1536]{0:T(1024)} %get-tuple-element.238) | copy-start | bytes 18436
  75.7 11.0 %copy-start.14 = (f32[1536]{0:T(1024)S(1)}, f32[1536]{0:T(1024)}, u32[]{:S(2)}) copy-start(f32[1536]{0:T(1024)} %get-tuple-element.239) | copy-start | bytes 18436
  75.7 11.0 %copy-start.15 = (f32[1536]{0:T(1024)S(1)}, f32[1536]{0:T(1024)}, u32[]{:S(2)}) copy-start(f32[1536]{0:T(1024)} %get-tuple-element.240) | copy-start | bytes 18436
  75.7 11.0 %copy-start.16 = (f32[1536]{0:T(1024)S(1)}, f32[1536]{0:T(1024)}, u32[]{:S(2)}) copy-start(f32[1536]{0:T(1024)} %get-tuple-element.241) | copy-start | bytes 18436
  75.7 11.0 %copy-start.17 = (f32[1536]{0:T(1024)S(1)}, f32[1536]{0:T(1024)}, u32[]{:S(2)}) copy-start(f32[1536]{0:T(1024)} %get-tuple-element.242) | copy-start | bytes 18436
  75.7 11.0 %copy-start.18 = (f32[1536]{0:T(1024)S(1)}, f32[1536]{0:T(1024)}, u32[]{:S(2)}) copy-start(f32[1536]{0:T(1024)} %get-tuple-element.243) | copy-start | bytes 18436
  78.6 4.9 %collective-permute-start = (bf16[15,1536]{1,0:T(8,128)(2,1)S(1)}, bf16[15,1536]{1,0:T(8,128)(2,1)S(1)}, u32[]{:S(2)}, u32[]{:S(2)}) collective-permute-start(bf16[15,1536]{1,0:T(8,128)(2,1)S(1)} %get-tuple-element.307), channel_id=1, source_target_pairs={{0,4},{4,8},{8,12},{12,16},{16,20},{20,24},{24,28},{1,5},{5,9},{9,... | collective-permute-start | bytes 138248 | tf_op jit(solution)/shard_map/ppermute | solution.py:21
  80.6 6.0 %collective-permute-start.1 = (bf16[15,1536]{1,0:T(8,128)(2,1)S(1)}, bf16[15,1536]{1,0:T(8,128)(2,1)S(1)}, u32[]{:S(2)}, u32[]{:S(2)}) collective-permute-start(bf16[15,1536]{1,0:T(8,128)(2,1)S(1)} %get-tuple-element.308), channel_id=1, source_target_pairs={{4,0},{8,4},{12,8},{16,12},{20,16},{24,20},{28,24},{5,1},{9,5},{13... | collective-permute-start | bytes 138248 | tf_op jit(solution)/shard_map/ppermute | solution.py:22
  94.4 6.7 %collective-permute-start.2 = (f32[15,1536]{1,0:T(8,128)S(1)}, f32[15,1536]{1,0:T(8,128)S(1)}, u32[]{:S(2)}, u32[]{:S(2)}) collective-permute-start(f32[15,1536]{1,0:T(8,128)S(1)} %get-tuple-element.305), channel_id=1, source_target_pairs={{4,0},{8,4},{12,8},{16,12},{20,16},{24,20},{28,24},{5,1},{9,5},{13... | collective-permute-start | bytes 276488 | tf_op jit(solution)/shard_map/ppermute | solution.py:22
  95.7 7.0 %collective-permute-start.3 = (f32[15,1536]{1,0:T(8,128)S(1)}, f32[15,1536]{1,0:T(8,128)S(1)}, u32[]{:S(2)}, u32[]{:S(2)}) collective-permute-start(f32[15,1536]{1,0:T(8,128)S(1)} %get-tuple-element.306), channel_id=1, source_target_pairs={{0,4},{4,8},{8,12},{12,16},{16,20},{20,24},{24,28},{1,5},{5,9},{9,... | collective-permute-start | bytes 276488 | tf_op jit(solution)/shard_map/ppermute | solution.py:21
  115.5 18.4 %all-to-all-start.4 = ((bf16[8,128,96]{1,2,0:T(8,128)(2,1)}), bf16[8,128,96]{1,2,0:T(8,128)(2,1)S(1)}, u32[]{:S(2)}, u32[]{:S(2)}) async-start(bf16[8,128,96]{1,2,0:T(8,128)(2,1)} %bitcast.121), calls=%async_computation.4 | async-start | bytes 393216 | tf_op jit(solution)/shard_map/all_to_all | solution.py:157
  122.2 154.4 %all-reduce.5.cloned.1.call-start = ((), (), s32[]{:S(2)}) async-start(), calls=%async_computation.9 | async-start | bytes 393216 | tf_op jit(solution)/shard_map/psum | solution.py:172
  125.4 11.2 %copy-start.2 = (bf16[1024,96]{1,0:T(8,128)(2,1)S(1)}, bf16[1024,96]{1,0:T(8,128)(2,1)}, u32[]{:S(2)}) copy-start(bf16[1024,96]{1,0:T(8,128)(2,1)} %copy-done.1) | copy-start | bytes 589828
  125.4 11.2 %copy-start.4 = (bf16[1024,96]{1,0:T(8,128)(2,1)S(1)}, bf16[1024,96]{1,0:T(8,128)(2,1)}, u32[]{:S(2)}) copy-start(bf16[1024,96]{1,0:T(8,128)(2,1)} %copy-done.3) | copy-start | bytes 589828
  125.4 11.2 %copy-start.6 = (bf16[2,512,96]{2,1,0:T(8,128)(2,1)S(1)}, bf16[2,512,96]{2,1,0:T(8,128)(2,1)}, u32[]{:S(2)}) copy-start(bf16[2,512,96]{2,1,0:T(8,128)(2,1)} %copy-done.5) | copy-start | bytes 589828
  149.4 64.9 %copy-start.9 = (f32[128,1536]{1,0:T(8,128)S(1)}, f32[128,1536]{1,0:T(8,128)}, u32[]{:S(2)}) copy-start(f32[128,1536]{1,0:T(8,128)} %get-tuple-element.300) | copy-start | bytes 2359300
  149.5 64.9 %copy-start.10 = (bf16[128,1536]{1,0:T(8,128)(2,1)S(1)}, bf16[128,1536]{1,0:T(8,128)(2,1)}, u32[]{:S(2)}) copy-start(bf16[128,1536]{1,0:T(8,128)(2,1)} %get-tuple-element.310) | copy-start | bytes 1179652
  149.5 64.9 %copy-start.51 = (pred[128]{0:T(512)(128)(4,1)S(1)}, pred[128]{0:T(512)(128)(4,1)}, u32[]{:S(2)}) copy-start(pred[128]{0:T(512)(128)(4,1)} %add_compare_fusion) | copy-start | bytes 388
  154.0 61.4 %copy-start.48 = (f32[1536]{0:T(1024)S(1)}, f32[1536]{0:T(1024)}, u32[]{:S(2)}) copy-start(f32[1536]{0:T(1024)} %get-tuple-element.235) | copy-start | bytes 18436
  159.8 118.3 %all-to-all-start.5 = ((bf16[8,2,6144]{2,1,0:T(2,128)(2,1)}), bf16[8,2,6144]{2,1,0:T(2,128)(2,1)}, u32[]{:S(2)}, u32[]{:S(2)}) async-start(bf16[8,2,6144]{2,1,0:T(2,128)(2,1)} %reshape.157), calls=%async_computation.5 | async-start | bytes 393216 | tf_op jit(solution)/shard_map/all_to_all | solution.py:165
  164.2 148.0 %all-reduce.3.cloned.1.call-start = ((), (), s32[]{:S(2)}) async-start(), calls=%async_computation.8 | async-start | bytes 589824 | tf_op jit(solution)/shard_map/psum | solution.py:171
  (35 other events, 218.9 us)
Sparse Core Ops, SparseCore 0:
  110.3 102.1 reduce-scatter.1
Sparse Core Ops, SparseCore 1:
  132.5 144.0 all-reduce.4
  279.3 32.9 all-reduce.2
where the time goes:
time: 324 us; the launch traced here: 322 us
  waiting for transfers between devices  130 us (40%)
  local copies, waits for them, and re-layouts  44.2 us (14%)
  blocking collectives  40.3 us (12%)
  starting transfers between devices  38.2 us (12%)
  other arithmetic  31.9 us (10%)
  matrix products  19.4 us (6%)
  between operations  17.3 us (5%)
    reduce_scatter x1, waiting for transfers between devices, on_device(): lax.psum_scatter(term_block, 'seq', scatter_dimension=0, tiled=True)  48.2 us
    psum x1, blocking collectives, on_device(): lax.psum((kernel_local, bias_local), ('seq', 'dp'))  40.3 us
    psum x1, waiting for transfers between devices, on_device(): lax.psum(partial_rows.astype(jnp.bfloat16), 'dp').astype(jnp.float32)  31.7 us
    psum x1, waiting for transfers between devices, on_device(): lax.psum((kernel_local, bias_local), ('seq', 'dp'))  20.2 us
    unnamed x119, local copies, waits for them, and re-layouts  15.6 us
    reduce_sum x2, other arithmetic, on_device(): jnp.sum(grad_conv * padded[tap:tap + frames_dev], axis=0)  10.5 us
    unnamed x2, other arithmetic  7.45 us
    all_to_all x1, waiting for transfers between devices, on_device(): lax.all_to_all(value_send, 'seq', split_axis=0, concat_axis=1, tiled=True)  7.34 us
  transfers between devices with their start and end apart: 13, of which 11 were waited for; matrix products, arithmetic and copies ran while one was open for 18% of the time, Pallas kernels for 0%

commit v1 on v0

--- a/solution.py
+++ b/solution.py
@@ -168,7 +168,9 @@
         grad_input, attended, (((0,), (0,)), ((), ())), preferred_element_type=jnp.float32
     )
     partial_rows = lax.psum_scatter(term_block, "seq", scatter_dimension=0, tiled=True)
-    summed = lax.psum(partial_rows.astype(jnp.bfloat16), "dp").astype(jnp.float32)
+    summed = jnp.sum(lax.all_gather(partial_rows.astype(jnp.bfloat16), "dp"), axis=0).astype(
+        jnp.float32
+    )
     kernel_total, bias_total = lax.psum((kernel_local, bias_local), ("seq", "dp"))
     shard_width = D // seq_count
     offset = lax.axis_index("seq") * shard_width

time: 324 us -> 300 us (0.926)
  waiting for transfers between devices: 130 us -> 106 us
    psum x1 -> x0, waiting for transfers between devices: 31.7 us -> none  [on_device(): lax.psum(partial_rows.astype(jnp.bfloat16), 'dp').astype(jnp.float32)]
    reduce_scatter x1, waiting for transfers between devices: 48.2 us -> 75.6 us  [on_device(): lax.psum_scatter(term_block, 'seq', scatter_dimension=0, tiled=True)]
    psum x1, waiting for transfers between devices: 20.2 us -> 0.01 us  [on_device(): lax.psum((kernel_local, bias_local), ('seq', 'dp'))]
  transfers between devices with their start and end apart: 13 -> 13, of which waited for: 11 -> 9; matrix products, arithmetic and copies ran while one was open for 18% -> 19% of each run, Pallas kernels for 0% -> 0%
where the time goes in v1:
time: 300 us; the launch traced here: 298 us
  waiting for transfers between devices  106 us (35%)
  local copies, waits for them, and re-layouts  44.2 us (15%)
  blocking collectives  40.8 us (14%)
  starting transfers between devices  38.2 us (13%)
  other arithmetic  32.5 us (11%)
  matrix products  19.2 us (6%)
  between operations  17.3 us (6%)
    reduce_scatter x1, waiting for transfers between devices, on_device(): lax.psum_scatter(term_block, 'seq', scatter_dimension=0, tiled=True)  75.6 us
    psum x1, blocking collectives, on_device(): lax.psum((kernel_local, bias_local), ('seq', 'dp'))  40.8 us
    unnamed x119, local copies, waits for them, and re-layouts  15.6 us
    reduce_sum x2, other arithmetic, on_device(): jnp.sum(grad_conv * padded[tap:tap + frames_dev], axis=0)  10.6 us
    unnamed x2, other arithmetic  7.44 us
    all_to_all x1, waiting for transfers between devices, on_device(): lax.all_to_all(value_send, 'seq', split_axis=0, concat_axis=1, tiled=True)  7.34 us
    all_to_all x1, starting transfers between devices, on_device(): lax.all_to_all(to_serving(query_local), 'seq', split_axis=0, concat_axis=...  7.28 us
    ppermute x2, starting transfers between devices, with_halo(): before = lax.ppermute(last, axis, up)  6.91 us
  transfers between devices with their start and end apart: 13, of which 9 were waited for; matrix products, arithmetic and copies ran while one was open for 19% of the time, Pallas kernels for 0%

profile of v1, /device:TPU:0, one launch (start us, length us, event | category | flops | bytes accessed | tf_op | source)
XLA Modules:
  0.0 297.8 jit_solution(16587339482942641711)
XLA Ops:
  9.9 7.3 %all-to-all-start = ((bf16[8,128,96]{1,2,0:T(8,128)(2,1)}), bf16[8,128,96]{1,2,0:T(8,128)(2,1)S(1)}, u32[]{:S(2)}, u32[]{:S(2)}) async-start(bf16[8,128,96]{1,2,0:T(8,128)(2,1)} %bitcast.3), calls=%async_computation | async-start | bytes 393216 | tf_op jit(solution)/shard_map/all_to_all | solution.py:107
  18.9 6.2 %all-to-all-done = bf16[8,128,96]{1,2,0:T(8,128)(2,1)S(1)} async-done(((bf16[8,128,96]{1,2,0:T(8,128)(2,1)}), bf16[8,128,96]{1,2,0:T(8,128)(2,1)S(1)}, u32[]{:S(2)}, u32[]{:S(2)}) %all-to-all-start) | async-done | bytes 196640 | tf_op jit(solution)/shard_map/all_to_all | solution.py:107
  25.1 3.4 %all-to-all-start.1 = ((bf16[8,128,96]{1,2,0:T(8,128)(2,1)}), bf16[8,128,96]{1,2,0:T(8,128)(2,1)S(1)}, u32[]{:S(2)}, u32[]{:S(2)}) async-start(bf16[8,128,96]{1,2,0:T(8,128)(2,1)} %bitcast.5), calls=%async_computation.1 | async-start | bytes 393216 | tf_op jit(solution)/shard_map/all_to_all | solution.py:117
  30.3 6.0 %all-to-all-done.1 = bf16[8,128,96]{1,2,0:T(8,128)(2,1)S(1)} async-done(((bf16[8,128,96]{1,2,0:T(8,128)(2,1)}), bf16[8,128,96]{1,2,0:T(8,128)(2,1)S(1)}, u32[]{:S(2)}, u32[]{:S(2)}) %all-to-all-start.1) | async-done | bytes 196640 | tf_op jit(solution)/shard_map/all_to_all | solution.py:117
  36.3 3.4 %all-to-all-start.2 = ((bf16[8,128,96]{1,2,0:T(8,128)(2,1)}), bf16[8,128,96]{1,2,0:T(8,128)(2,1)S(1)}, u32[]{:S(2)}, u32[]{:S(2)}) async-start(bf16[8,128,96]{1,2,0:T(8,128)(2,1)} %bitcast.7), calls=%async_computation.2 | async-start | bytes 393216 | tf_op jit(solution)/shard_map/all_to_all | solution.py:118
  40.0 7.3 %all-to-all-done.2 = bf16[8,128,96]{1,2,0:T(8,128)(2,1)S(1)} async-done(((bf16[8,128,96]{1,2,0:T(8,128)(2,1)}), bf16[8,128,96]{1,2,0:T(8,128)(2,1)S(1)}, u32[]{:S(2)}, u32[]{:S(2)}) %all-to-all-start.2) | async-done | bytes 196640 | tf_op jit(solution)/shard_map/all_to_all | solution.py:118
  47.6 4.6 %while.24 = (s32[]{:T(128)}, bf16[2,512,96]{1,2,0:T(8,128)(2,1)S(1)}, f32[2,512]{1,0:T(2,128)S(1)}, bf16[2,512,96]{2,1,0:T(8,128)(2,1)S(1)}, bf16[1024,96]{1,0:T...) while((s32[]{:T(128)}, ...), condition=%wide.region_3.4_spmd.clone, body=%wide.region_0.3_spmd.clone.sunk | while | flops 204997120 | bytes 7164021 | solution.py:45
  53.2 2.6 reshape.123
  56.3 3.7 %reduce.64 = bf16[1024,96]{1,0:T(8,128)(2,1)} reduce(bf16[1024,1,96]{2,1,0:T(2,128)(2,1)} %bitcast.116, bf16[]{:T(256)} %broadcast.73), dimensions={1}, to_apply=%bitcast.67.reduce_sub_computation | reduce | bytes 393218
  60.0 2.1 reshape.156
  62.1 3.4 %all-to-all-start.3 = ((bf16[8,2,6144]{2,1,0:T(2,128)(2,1)}), bf16[8,2,6144]{2,1,0:T(2,128)(2,1)S(1)}, u32[]{:S(2)}, u32[]{:S(2)}) async-start(bf16[8,2,6144]{2,1,0:T(2,128)(2,1)} %reshape.156), calls=%async_computation.3 | async-start | bytes 393216 | tf_op jit(solution)/shard_map/all_to_all | solution.py:125
  66.8 2.5 slice_reduce_fusion.30
  69.3 4.0 %all-to-all-done.3 = bf16[8,2,6144]{2,1,0:T(2,128)(2,1)S(1)} async-done(((bf16[8,2,6144]{2,1,0:T(2,128)(2,1)}), bf16[8,2,6144]{2,1,0:T(2,128)(2,1)S(1)}, u32[]{:S(2)}, u32[]{:S(2)}) %all-to-all-start.3) | async-done | bytes 196640 | tf_op jit(solution)/shard_map/all_to_all | solution.py:125
  75.9 2.7 broadcast_select_fusion
  83.5 3.0 %collective-permute-done.1 = bf16[15,1536]{1,0:T(8,128)(2,1)S(1)} collective-permute-done((bf16[15,1536]{1,0:T(8,128)(2,1)S(1)}, bf16[15,1536]{1,0:T(8,128)(2,1)S(1)}, u32[]{:S(2)}, u32[]{:S(2)}) %collective-permute-start.1) | collective-permute-done | bytes 46112 | tf_op jit(solution)/shard_map/ppermute | solution.py:22
  86.9 7.5 %multiply_reduce_fusion = (f32[1536]{0:T(1024)}, f32[1536]{0:T(1024)}, f32[1536]{0:T(1024)}, f32[1536]{0:T(1024)}, f32[1536]{0:T(1024)}, /*index=5*/f32[1536]{0:...) fusion(f32[158,1536]{1,0:T(8,128)S(1)} %maximum_convert_fusion,, ...), kind=kLoop, calls=%fused_computation.190 | loop fusion | flops 21206016 | bytes 26652800 | tf_op jit(solution)/shard_map/reduce_sum | solution.py:143
  95.7 5.0 %collective-permute-start.3 = (f32[15,1536]{1,0:T(8,128)S(1)}, f32[15,1536]{1,0:T(8,128)S(1)}, u32[]{:S(2)}, u32[]{:S(2)}) collective-permute-start(f32[15,1536]{1,0:T(8,128)S(1)} %get-tuple-element.306), channel_id=1, source_target_pairs={{0,4},{4,8},{8,12},{12,16},{16,20},{20,24},{24,28},{1,5},{5,9},{9,... | collective-permute-start | bytes 276488 | tf_op jit(solution)/shard_map/ppermute | solution.py:21
  102.7 3.7 %fusion.37 = bf16[128,1536]{1,0:T(8,128)(2,1)S(1)} fusion(f32[128,1536]{1,0:T(8,128)S(1)} %get-tuple-element.299, f32[15,1536]{1,0:T(8,128)S(1)} %collective-permute-done.3, f32[15,1536]{1,0:T(8,128)S(1)} %collective-permute-done.2, bf16[1,128,1536]{2,1,0:T(8,128)(2,1)S(1)} %copy-done.11, f32[1536]{0:T(1024)S(1)} %get-tuple-element.265, ...), kind=kLoop, calls=%fused_computation.100 | loop fusion | flops 18874368 | bytes 1947776 | tf_op jit(solution)/shard_map/convert_element_type | solution.py:151
  107.2 2.9 fusion.130
  111.1 2.1 reshape.121
  115.5 6.7 %all-to-all-start.4 = ((bf16[8,128,96]{1,2,0:T(8,128)(2,1)}), bf16[8,128,96]{1,2,0:T(8,128)(2,1)S(1)}, u32[]{:S(2)}, u32[]{:S(2)}) async-start(bf16[8,128,96]{1,2,0:T(8,128)(2,1)} %bitcast.123), calls=%async_computation.4 | async-start | bytes 393216 | tf_op jit(solution)/shard_map/all_to_all | solution.py:157
  122.4 3.0 %multiply_reduce_fusion.18 = (f32[1536]{0:T(1024)S(1)}, f32[1536]{0:T(1024)S(1)}, f32[1536]{0:T(1024)S(1)}, f32[1536]{0:T(1024)S(1)}, f32[1536]{0:T(1024)S(1)}, ...) fusion(f32[128,1536]{1,0:T(8,128)} %copy-done.7, ...), kind=kLoop, calls=%fused_computation.208 | loop fusion | flops 5286912 | bytes 11096064 | tf_op jit(solution)/shard_map/reduce_sum | solution.py:143
  128.9 3.5 %stack.127 = f32[31,1536]{1,0:T(8,128)} concatenate(f32[1,1536]{1,0:T(1,128)} %stack.96, f32[1,1536]{1,0:T(1,128)} %stack.97, f32[1,1536]{1,0:T(1,128)} %stack.98, f32[1,1536]{1,0:T(1,128)} %stack.99, f32[1,1536]{1,0:T(1,128)} %stack.100, f32[1,1536]{1,0:T(1,128)S(1)} %stack.101, f32[1,1536]{1,0:T(1,128)S(1)} %stack.102, f32[1,1536]{1,0:T(1,128)S(1)} %stack.103, ...), dimensions={0} | concatenate | bytes 380928 | tf_op jit(solution)/shard_map/stack | solution.py:142
  135.9 75.6 %reduce-scatter.2.cloned.1.call-done = f32[192,768]{1,0:T(8,128)} async-done(((f32[1536,768]{1,0:T(8,128)}), f32[192,768]{1,0:T(8,128)}) %reduce-scatter.2.cloned.1.call-update) | async-done | bytes 589840 | tf_op jit(solution)/shard_map/reduce_scatter | solution.py:170
  214.0 12.8 %while.25 = (s32[]{:T(128)}, bf16[2,512,96]{1,2,0:T(8,128)(2,1)}, bf16[2,512,96]{2,1,0:T(8,128)(2,1)S(1)}, bf16[1024,96]{1,0:T(8,128)(2,1)S(1)}, f32[2,512]{1,0:...) while((s32[]{:T(128)}, bf16[2,512,96]{1,2,0:T(8,128)(2,1)}, ...), condition=%wide.region_6.7_spmd.clone, body=%wide.region_5.6_spmd.clone.sunk | while | flops 305185792 | bytes 6241429 | solution.py:73
  217.2 3.2 %fusion.163 = bf16[2,512,96]{1,2,0:T(8,128)(2,1)} fusion(bf16[2,512,96]{1,2,0:T(8,128)(2,1)} %get-tuple-element.455, s32[]{:T(128)S(6)} %copy.133, bf16[1024,96]{1,0:T(8,128)(2,1)S(1)} %get-tuple-element.467, f32[512,1024]{1,0:T(8,128)} %fusion.162, bf16[1024,96]{1,0:T(8,128)(2,1)S(1)} %get-tuple-element.470, f32[512]{0:T(512)S(1)} %bitcast.131, ...), kind=kOutput, calls=%fused_computation.17.clone.1 | convolution fusion | flops 204521472 | bytes 2955264 | tf_op jit(solution)/shard_map/while/body/eval_jaxpr/dot_general | solution.py:71
  223.6 3.2 %fusion.163 = bf16[2,512,96]{1,2,0:T(8,128)(2,1)} fusion(bf16[2,512,96]{1,2,0:T(8,128)(2,1)} %get-tuple-element.455, s32[]{:T(128)S(6)} %copy.133, bf16[1024,96]{1,0:T(8,128)(2,1)S(1)} %get-tuple-element.467, f32[512,1024]{1,0:T(8,128)} %fusion.162, bf16[1024,96]{1,0:T(8,128)(2,1)S(1)} %get-tuple-element.470, f32[512]{0:T(512)S(1)} %bitcast.131, ...), kind=kOutput, calls=%fused_computation.17.clone.1 | convolution fusion | flops 204521472 | bytes 2955264 | tf_op jit(solution)/shard_map/while/body/eval_jaxpr/dot_general | solution.py:71
  228.6 2.6 reshape.124
  231.2 3.7 %reduce.65 = bf16[1024,96]{1,0:T(8,128)(2,1)} reduce(bf16[1024,1,96]{2,1,0:T(2,128)(2,1)} %bitcast.117, bf16[]{:T(256)} %broadcast.73), dimensions={1}, to_apply=%bitcast.69.reduce_sub_computation | reduce | bytes 393218
  235.0 2.1 reshape.158
  237.0 4.5 %all-to-all-start.5 = ((bf16[8,2,6144]{2,1,0:T(2,128)(2,1)}), bf16[8,2,6144]{2,1,0:T(2,128)(2,1)}, u32[]{:S(2)}, u32[]{:S(2)}) async-start(bf16[8,2,6144]{2,1,0:T(2,128)(2,1)} %reshape.158), calls=%async_computation.5 | async-start | bytes 393216 | tf_op jit(solution)/shard_map/all_to_all | solution.py:165
  242.6 40.8 %psum.15 = f32[1536]{0:T(1024)S(1)} all-reduce(f32[1536]{0:T(1024)S(1)} %copy-done.48), channel_id=1, replica_groups=mesh['seq'=8,'dp'=4] {'seq','dp'}, use_global_device_ids=true, to_apply=%region_42.43 | all-reduce | flops 1536 | bytes 12288 | tf_op jit(solution)/shard_map/psum | solution.py:174
  (211 shorter events, 52.8 us)
Async XLA Ops:
  8.0 67.6 %copy-start = (bf16[1536,768]{1,0:T(8,128)(2,1)S(1)}, bf16[1536,768]{1,0:T(8,128)(2,1)}, u32[]{:S(2)}) copy-start(bf16[1536,768]{1,0:T(8,128)(2,1)} %param.18) | copy-start | bytes 7077892
  9.9 15.2 %all-to-all-start = ((bf16[8,128,96]{1,2,0:T(8,128)(2,1)}), bf16[8,128,96]{1,2,0:T(8,128)(2,1)S(1)}, u32[]{:S(2)}, u32[]{:S(2)}) async-start(bf16[8,128,96]{1,2,0:T(8,128)(2,1)} %bitcast.3), calls=%async_computation | async-start | bytes 393216 | tf_op jit(solution)/shard_map/all_to_all | solution.py:107
  25.1 11.1 %all-to-all-start.1 = ((bf16[8,128,96]{1,2,0:T(8,128)(2,1)}), bf16[8,128,96]{1,2,0:T(8,128)(2,1)S(1)}, u32[]{:S(2)}, u32[]{:S(2)}) async-start(bf16[8,128,96]{1,2,0:T(8,128)(2,1)} %bitcast.5), calls=%async_computation.1 | async-start | bytes 393216 | tf_op jit(solution)/shard_map/all_to_all | solution.py:117
  36.3 11.1 %all-to-all-start.2 = ((bf16[8,128,96]{1,2,0:T(8,128)(2,1)}), bf16[8,128,96]{1,2,0:T(8,128)(2,1)S(1)}, u32[]{:S(2)}, u32[]{:S(2)}) async-start(bf16[8,128,96]{1,2,0:T(8,128)(2,1)} %bitcast.7), calls=%async_computation.2 | async-start | bytes 393216 | tf_op jit(solution)/shard_map/all_to_all | solution.py:118
  52.2 14.0 %copy-start.49 = (f32[2,512]{1,0:T(2,128)}, f32[2,512]{1,0:T(2,128)S(1)}, u32[]{:S(2)}) copy-start(f32[2,512]{1,0:T(2,128)S(1)} %get-tuple-element.448) | copy-start | bytes 12292
  52.3 23.3 %copy-start.1 = (bf16[1024,96]{1,0:T(8,128)(2,1)}, bf16[1024,96]{1,0:T(8,128)(2,1)S(1)}, u32[]{:S(2)}) copy-start(bf16[1024,96]{1,0:T(8,128)(2,1)S(1)} %get-tuple-element.477) | copy-start | bytes 589828
  52.3 23.3 %copy-start.3 = (bf16[1024,96]{1,0:T(8,128)(2,1)}, bf16[1024,96]{1,0:T(8,128)(2,1)S(1)}, u32[]{:S(2)}) copy-start(bf16[1024,96]{1,0:T(8,128)(2,1)S(1)} %get-tuple-element.480) | copy-start | bytes 589828
  52.3 23.3 %copy-start.5 = (bf16[2,512,96]{2,1,0:T(8,128)(2,1)}, bf16[2,512,96]{2,1,0:T(8,128)(2,1)S(1)}, u32[]{:S(2)}) copy-start(bf16[2,512,96]{2,1,0:T(8,128)(2,1)S(1)} %get-tuple-element.481) | copy-start | bytes 589828
  62.1 11.1 %all-to-all-start.3 = ((bf16[8,2,6144]{2,1,0:T(2,128)(2,1)}), bf16[8,2,6144]{2,1,0:T(2,128)(2,1)S(1)}, u32[]{:S(2)}, u32[]{:S(2)}) async-start(bf16[8,2,6144]{2,1,0:T(2,128)(2,1)} %reshape.156), calls=%async_computation.3 | async-start | bytes 393216 | tf_op jit(solution)/shard_map/all_to_all | solution.py:125
  65.5 145.9 %reduce-scatter.2.cloned.1.call-start = ((), (), s32[]{:S(2)}) async-start(), calls=%async_computation.7 | async-start | bytes 5308416 | tf_op jit(solution)/shard_map/reduce_scatter | solution.py:170
  75.6 11.0 %copy-start.11 = (bf16[1,128,1536]{2,1,0:T(8,128)(2,1)S(1)}, bf16[1,128,1536]{2,1,0:T(8,128)(2,1)}, u32[]{:S(2)}) copy-start(bf16[1,128,1536]{2,1,0:T(8,128)(2,1)} %param.21) | copy-start | bytes 1179652
  75.7 11.0 %copy-start.13 = (f32[1536]{0:T(1024)S(1)}, f32[1536]{0:T(1024)}, u32[]{:S(2)}) copy-start(f32[1536]{0:T(1024)} %get-tuple-element.238) | copy-start | bytes 18436
  75.7 11.0 %copy-start.14 = (f32[1536]{0:T(1024)S(1)}, f32[1536]{0:T(1024)}, u32[]{:S(2)}) copy-start(f32[1536]{0:T(1024)} %get-tuple-element.239) | copy-start | bytes 18436
  75.7 11.0 %copy-start.15 = (f32[1536]{0:T(1024)S(1)}, f32[1536]{0:T(1024)}, u32[]{:S(2)}) copy-start(f32[1536]{0:T(1024)} %get-tuple-element.240) | copy-start | bytes 18436
  75.7 11.0 %copy-start.16 = (f32[1536]{0:T(1024)S(1)}, f32[1536]{0:T(1024)}, u32[]{:S(2)}) copy-start(f32[1536]{0:T(1024)} %get-tuple-element.241) | copy-start | bytes 18436
  75.7 11.0 %copy-start.17 = (f32[1536]{0:T(1024)S(1)}, f32[1536]{0:T(1024)}, u32[]{:S(2)}) copy-start(f32[1536]{0:T(1024)} %get-tuple-element.242) | copy-start | bytes 18436
  75.7 11.0 %copy-start.18 = (f32[1536]{0:T(1024)S(1)}, f32[1536]{0:T(1024)}, u32[]{:S(2)}) copy-start(f32[1536]{0:T(1024)} %get-tuple-element.243) | copy-start | bytes 18436
  78.6 4.9 %collective-permute-start = (bf16[15,1536]{1,0:T(8,128)(2,1)S(1)}, bf16[15,1536]{1,0:T(8,128)(2,1)S(1)}, u32[]{:S(2)}, u32[]{:S(2)}) collective-permute-start(bf16[15,1536]{1,0:T(8,128)(2,1)S(1)} %get-tuple-element.307), channel_id=1, source_target_pairs={{0,4},{4,8},{8,12},{12,16},{16,20},{20,24},{24,28},{1,5},{5,9},{9,... | collective-permute-start | bytes 138248 | tf_op jit(solution)/shard_map/ppermute | solution.py:21
  80.6 6.0 %collective-permute-start.1 = (bf16[15,1536]{1,0:T(8,128)(2,1)S(1)}, bf16[15,1536]{1,0:T(8,128)(2,1)S(1)}, u32[]{:S(2)}, u32[]{:S(2)}) collective-permute-start(bf16[15,1536]{1,0:T(8,128)(2,1)S(1)} %get-tuple-element.308), channel_id=1, source_target_pairs={{4,0},{8,4},{12,8},{16,12},{20,16},{24,20},{28,24},{5,1},{9,5},{13... | collective-permute-start | bytes 138248 | tf_op jit(solution)/shard_map/ppermute | solution.py:22
  94.4 6.7 %collective-permute-start.2 = (f32[15,1536]{1,0:T(8,128)S(1)}, f32[15,1536]{1,0:T(8,128)S(1)}, u32[]{:S(2)}, u32[]{:S(2)}) collective-permute-start(f32[15,1536]{1,0:T(8,128)S(1)} %get-tuple-element.305), channel_id=1, source_target_pairs={{4,0},{8,4},{12,8},{16,12},{20,16},{24,20},{28,24},{5,1},{9,5},{13... | collective-permute-start | bytes 276488 | tf_op jit(solution)/shard_map/ppermute | solution.py:22
  95.7 7.0 %collective-permute-start.3 = (f32[15,1536]{1,0:T(8,128)S(1)}, f32[15,1536]{1,0:T(8,128)S(1)}, u32[]{:S(2)}, u32[]{:S(2)}) collective-permute-start(f32[15,1536]{1,0:T(8,128)S(1)} %get-tuple-element.306), channel_id=1, source_target_pairs={{0,4},{4,8},{8,12},{12,16},{16,20},{20,24},{24,28},{1,5},{5,9},{9,... | collective-permute-start | bytes 276488 | tf_op jit(solution)/shard_map/ppermute | solution.py:21
  115.5 18.4 %all-to-all-start.4 = ((bf16[8,128,96]{1,2,0:T(8,128)(2,1)}), bf16[8,128,96]{1,2,0:T(8,128)(2,1)S(1)}, u32[]{:S(2)}, u32[]{:S(2)}) async-start(bf16[8,128,96]{1,2,0:T(8,128)(2,1)} %bitcast.123), calls=%async_computation.4 | async-start | bytes 393216 | tf_op jit(solution)/shard_map/all_to_all | solution.py:157
  122.2 161.8 %all-reduce.2.cloned.1.call-start = ((), (), s32[]{:S(2)}) async-start(), calls=%async_computation.8 | async-start | bytes 393216 | tf_op jit(solution)/shard_map/psum | solution.py:174
  125.4 88.6 %copy-start.2 = (bf16[1024,96]{1,0:T(8,128)(2,1)S(1)}, bf16[1024,96]{1,0:T(8,128)(2,1)}, u32[]{:S(2)}) copy-start(bf16[1024,96]{1,0:T(8,128)(2,1)} %copy-done.1) | copy-start | bytes 589828
  125.4 88.6 %copy-start.4 = (bf16[1024,96]{1,0:T(8,128)(2,1)S(1)}, bf16[1024,96]{1,0:T(8,128)(2,1)}, u32[]{:S(2)}) copy-start(bf16[1024,96]{1,0:T(8,128)(2,1)} %copy-done.3) | copy-start | bytes 589828
  125.4 88.6 %copy-start.6 = (bf16[2,512,96]{2,1,0:T(8,128)(2,1)S(1)}, bf16[2,512,96]{2,1,0:T(8,128)(2,1)}, u32[]{:S(2)}) copy-start(bf16[2,512,96]{2,1,0:T(8,128)(2,1)} %copy-done.5) | copy-start | bytes 589828
  132.4 155.6 %all-gather.3.cloned.1.call-start = ((), (), s32[]{:S(2)}) async-start(), calls=%async_computation.9 | async-start | bytes 1474560 | tf_op jit(solution)/shard_map/all_gather | solution.py:171
  226.7 14.8 %copy-start.9 = (f32[128,1536]{1,0:T(8,128)S(1)}, f32[128,1536]{1,0:T(8,128)}, u32[]{:S(2)}) copy-start(f32[128,1536]{1,0:T(8,128)} %get-tuple-element.300) | copy-start | bytes 2359300
  226.7 14.8 %copy-start.10 = (bf16[128,1536]{1,0:T(8,128)(2,1)S(1)}, bf16[128,1536]{1,0:T(8,128)(2,1)}, u32[]{:S(2)}) copy-start(bf16[128,1536]{1,0:T(8,128)(2,1)} %get-tuple-element.310) | copy-start | bytes 1179652
  226.8 14.8 %copy-start.51 = (pred[128]{0:T(512)(128)(4,1)S(1)}, pred[128]{0:T(512)(128)(4,1)}, u32[]{:S(2)}) copy-start(pred[128]{0:T(512)(128)(4,1)} %add_compare_fusion) | copy-start | bytes 388
  228.6 14.0 %copy-start.48 = (f32[1536]{0:T(1024)S(1)}, f32[1536]{0:T(1024)}, u32[]{:S(2)}) copy-start(f32[1536]{0:T(1024)} %get-tuple-element.235) | copy-start | bytes 18436
  237.0 48.5 %all-to-all-start.5 = ((bf16[8,2,6144]{2,1,0:T(2,128)(2,1)}), bf16[8,2,6144]{2,1,0:T(2,128)(2,1)}, u32[]{:S(2)}, u32[]{:S(2)}) async-start(bf16[8,2,6144]{2,1,0:T(2,128)(2,1)} %reshape.158), calls=%async_computation.5 | async-start | bytes 393216 | tf_op jit(solution)/shard_map/all_to_all | solution.py:165
  (35 other events, 218.9 us)
Sparse Core Ops, SparseCore 0:
  110.3 101.0 reduce-scatter.1
  213.4 17.3 all-gather.2
Sparse Core Ops, SparseCore 1:
  132.5 142.2 all-reduce.1
